TPU v7x, 32 devices: a whole 2x2x4 slice. The times are simulated.
32 devices in a mesh: row: 8 (over z, x), col: 4 (over y, core).
Axes of the slice: x: 2, y: 2, z: 4, core: 2. Of those that a mesh axis runs over, the one named last changes fastest.
Arguments:
- mom_a: float32 [1536, 12288], P('row', 'col'), may hold values from -6 to 6
- grad_a: float32 [1536, 12288], P('row', 'col'), may hold values from -6 to 6
- basis_a: float32 [512, 12288], P('row', 'col'), may hold values from -0.0546875 to 0.0546875
- mom_b: float32 [7168, 1536], P('row', 'col'), may hold values from -6 to 6
- grad_b: float32 [7168, 1536], P('row', 'col'), may hold values from -6 to 6
- basis_b: float32 [512, 1536], P('row', 'col'), may hold values from -0.15625 to 0.15625
Outputs:
- new_mom_a: float32 [1536, 12288], P('row', 'col')
- update_a: bfloat16 [1536, 12288], P('row', 'col')
- new_basis_a: float32 [512, 12288], P('row', 'col')
- new_mom_b: float32 [7168, 1536], P('row', 'col')
- update_b: bfloat16 [7168, 1536], P('row', 'col')
- new_basis_b: float32 [512, 1536], P('row', 'col')
All inputs are finite; a program needn't handle non-finite values.
Results may differ from a plain program's by a relative error of at most 0.0049.
Values sent between devices are 32-bit elements; how exact they have to be, the bound alone decides.
A program may use at most 128 MiB of HBM per device.

v0:
```python
import math
import jax
import jax.numpy as jnp
from jax import lax
from jax.sharding import PartitionSpec as P

MU = 0.95
EPS = 1e-06


def project(buffer, basis):
    partial_proj = jnp.dot(
        buffer,
        lax.all_gather(basis, "row", axis=0, tiled=True).T,
        precision=lax.Precision.HIGHEST,
        preferred_element_type=jnp.float32,
    )
    return lax.psum(partial_proj, "col")


def local_gram(proj):
    return jnp.dot(
        proj.T, proj, precision=lax.Precision.HIGHEST, preferred_element_type=jnp.float32
    )


def single_gram(proj):
    return lax.psum(local_gram(proj), "row")


def finish(buffer, proj, gram):
    highest = lax.Precision.HIGHEST
    lower = jnp.linalg.cholesky(gram)
    ortho = lax.linalg.triangular_solve(lower, proj, left_side=False, lower=True, transpose_a=True)
    rank = ortho.shape[1]
    share_rows = rank // lax.axis_size("row")
    trans = lax.psum(
        jnp.dot(ortho.T, buffer, precision=highest, preferred_element_type=jnp.float32), "row"
    )
    squares = lax.psum(jnp.sum(trans * trans, axis=1, keepdims=True), "col")
    full_basis = trans / jnp.sqrt(squares + EPS)
    own_basis = lax.dynamic_slice_in_dim(
        full_basis, lax.axis_index("row") * share_rows, share_rows, 0
    )
    new_mom = buffer - (1.0 - MU) * jnp.dot(
        ortho, trans, precision=highest, preferred_element_type=jnp.float32
    )
    total_rows = buffer.shape[0] * lax.axis_size("row")
    total_cols = buffer.shape[1] * lax.axis_size("col")
    scale = math.sqrt(total_rows * total_cols / rank)
    update = (
        jnp.dot(ortho, full_basis, precision=highest, preferred_element_type=jnp.float32) * scale
    ).astype(jnp.bfloat16)
    return (new_mom, update, own_basis)


def shards(mom_a, grad_a, basis_a, mom_b, grad_b, basis_b):
    buffers = [MU * mom_a + grad_a, MU * mom_b + grad_b]
    projs = [project(buffers[0], basis_a), project(buffers[1], basis_b)]
    grams = [single_gram(projs[0]), single_gram(projs[1])]
    first = finish(buffers[0], projs[0], grams[0])
    second = finish(buffers[1], projs[1], grams[1])
    return (first[0], first[1], first[2], second[0], second[1], second[2])


def solution(mesh):
    return jax.shard_map(
        shards,
        mesh=mesh,
        in_specs=(
            P("row", "col"),
            P("row", "col"),
            P("row", "col"),
            P("row", "col"),
            P("row", "col"),
            P("row", "col"),
        ),
        out_specs=(
            P("row", "col"),
            P("row", "col"),
            P("row", "col"),
            P("row", "col"),
            P("row", "col"),
            P("row", "col"),
        ),
        check_vma=False,
    )
```

profile of v0, /device:TPU:0, one launch (start us, length us, event | category | flops | bytes accessed | tf_op | source)
XLA Modules:
  0.0 905.2 jit_solution(12628159477295165180)
XLA Ops:
  7.9 36.6 %all_gather.7 = f32[512,384]{1,0:T(8,128)S(1)} all-gather(f32[64,384]{1,0:T(8,128)} %param.12), channel_id=1, replica_groups=mesh['row'=8,'col'=4] {'row'}, dimensions={0}, use_global_device_ids=true | all-gather | bytes 884736 | tf_op jit(solution)/shard_map/all_gather | solution.py:14
  44.6 6.2 fusion.76
  50.8 65.1 %all-gather.2.cloned.1.call-done = f32[512,3072]{1,0:T(8,128)} async-done(((f32[64,3072]{1,0:T(8,128)}), f32[512,3072]{1,0:T(8,128)}) %all-gather.2.cloned.1.call-update) | async-done | bytes 6291472 | tf_op jit(solution)/shard_map/all_gather | solution.py:14
  115.9 10.7 %fusion.77 = f32[192,512]{1,0:T(8,128)} fusion(f32[512,3072]{1,0:T(8,128)} %all-gather.2.cloned.1.call-done, f32[192,3072]{1,0:T(8,128)S(1)} %copy-done.1, f32[192,3072]{1,0:T(8,128)} %param.7), kind=kOutput, calls=%fused_computation.156 | convolution fusion | flops 3625058304 | bytes 11403264 | tf_op jit(solution)/shard_map/dot_general | solution.py:12
  126.6 11.9 %all-reduce.11.cloned.1.call-start = ((), (), s32[]{:S(2)}) async-start(), calls=%async_computation.2 | async-start | bytes 4194304 | tf_op jit(solution)/shard_map/psum | solution.py:28
  138.5 40.0 %all-reduce.13.cloned.1.call-done = (f32[192,512]{1,0:T(8,128)}, f32[896,512]{1,0:T(8,128)}) async-done(((f32[192,512]{1,0:T(8,128)}, f32[896,512]{1,0:T(8,128)}), (f32[192,512]{1,0:T(8,128)}, f32[896,512]{1,0:T(8,128)})) %all-reduce.13.cloned.1.call-update) | async-done | bytes 2228240 | tf_op jit(solution)/shard_map/psum | solution.py:18
  186.4 102.5 %all-reduce.11.cloned.1.call-done = (f32[512,512]{0,1:T(8,128)}, f32[512,512]{0,1:T(8,128)}) async-done(((f32[512,512]{0,1:T(8,128)}, f32[512,512]{0,1:T(8,128)}), (f32[512,512]{0,1:T(8,128)}, f32[512,512]{0,1:T(8,128)})) %all-reduce.11.cloned.1.call-update) | async-done | bytes 2097168 | tf_op jit(solution)/shard_map/psum | solution.py:28
  298.3 11.7 %cholesky.358 = f32[128,128]{1,0:T(8,128)S(1)} custom-call(f32[128,128]{1,0:T(8,128)S(1)} %cholesky.439), custom_call_target="Cholesky" | custom-call | tf_op jit(solution)/shard_map/jit(cholesky)/cholesky | solution.py:33
  310.1 9.8 %custom-call.34 = f32[1,128,128]{1,2,0:T(8,128)S(1)} custom-call(f32[1,128,128]{2,1,0:T(8,128)S(1)} %get-tuple-element.60), custom_call_target="InvertDiagBlocksLowerTriangular" | custom-call | tf_op jit(solution)/shard_map/jit(cholesky)/cholesky | solution.py:33
  323.2 11.7 %cholesky.377 = f32[128,128]{1,0:T(8,128)S(1)} custom-call(f32[128,128]{1,0:T(8,128)S(1)} %cholesky.443), custom_call_target="Cholesky" | custom-call | tf_op jit(solution)/shard_map/jit(cholesky)/cholesky | solution.py:33
  336.2 10.2 %custom-call.35 = f32[1,128,128]{1,2,0:T(8,128)S(1)} custom-call(f32[1,128,128]{2,1,0:T(8,128)S(1)} %get-tuple-element.57), custom_call_target="InvertDiagBlocksLowerTriangular" | custom-call | tf_op jit(solution)/shard_map/jit(cholesky)/cholesky | solution.py:33
  349.5 13.2 %cholesky.398 = f32[128,128]{1,0:T(8,128)} custom-call(f32[128,128]{1,0:T(8,128)} %cholesky.448), custom_call_target="Cholesky" | custom-call | tf_op jit(solution)/shard_map/jit(cholesky)/cholesky | solution.py:33
  364.9 11.3 %custom-call.36 = f32[1,128,128]{1,2,0:T(8,128)} custom-call(f32[1,128,128]{2,1,0:T(8,128)} %get-tuple-element.54), custom_call_target="InvertDiagBlocksLowerTriangular" | custom-call | tf_op jit(solution)/shard_map/jit(cholesky)/cholesky | solution.py:33
  378.5 11.9 %cholesky.415 = f32[128,128]{1,0:T(8,128)S(1)} custom-call(f32[128,128]{1,0:T(8,128)S(1)} %convolution_subtract_fusion.9), custom_call_target="Cholesky" | custom-call | tf_op jit(solution)/shard_map/jit(cholesky)/cholesky | solution.py:33
  394.7 11.6 %while.3 = (s32[]{:T(128)}, f32[512,512]{1,0:T(8,128)}, s32[4,2]{0,1:T(2,128)S(1)}, f32[4,128,128]{2,1,0:T(8,128)S(1)}, s32[]{:T(128)}) while((s32[]{:T(128)}, f32[512,512]{1,0:T(8,128)}, s32[4,2]{0,1:T(2,128)S(1)}, f32[4,128,128]{2,1,0:T(8,128)S(1)}, s32[]{:T(128)}) %tuple.56), condition=%wide.while_cond.1, body=%wide.while_body.1.sunk | while | flops 2 | bytes 131181 | solution.py:34
  406.3 39.3 %custom-call.27 = f32[4,128,128]{1,2,0:T(8,128)S(1)} custom-call(f32[4,128,128]{2,1,0:T(8,128)S(1)} %get-tuple-element.22), custom_call_target="InvertDiagBlocksLowerTriangular" | custom-call | tf_op jit(solution)/shard_map/triangular_solve | solution.py:34
  462.4 12.1 %cholesky.286 = f32[128,128]{1,0:T(8,128)S(1)} custom-call(f32[128,128]{1,0:T(8,128)S(1)} %cholesky.426), custom_call_target="Cholesky" | custom-call | tf_op jit(solution)/shard_map/jit(cholesky)/cholesky | solution.py:33
  474.5 9.8 %custom-call.31 = f32[1,128,128]{1,2,0:T(8,128)S(1)} custom-call(f32[1,128,128]{2,1,0:T(8,128)S(1)} %get-tuple-element.70), custom_call_target="InvertDiagBlocksLowerTriangular" | custom-call | tf_op jit(solution)/shard_map/jit(cholesky)/cholesky | solution.py:33
  488.6 12.3 %cholesky.305 = f32[128,128]{1,0:T(8,128)} custom-call(f32[128,128]{1,0:T(8,128)S(1)} %cholesky.430), custom_call_target="Cholesky" | custom-call | tf_op jit(solution)/shard_map/jit(cholesky)/cholesky | solution.py:33
  503.8 10.4 %custom-call.32 = f32[1,128,128]{1,2,0:T(8,128)} custom-call(f32[1,128,128]{2,1,0:T(8,128)S(1)} %get-tuple-element.67), custom_call_target="InvertDiagBlocksLowerTriangular" | custom-call | tf_op jit(solution)/shard_map/jit(cholesky)/cholesky | solution.py:33
  517.5 11.9 %cholesky.326 = f32[128,128]{1,0:T(8,128)S(1)} custom-call(f32[128,128]{1,0:T(8,128)S(1)} %cholesky.435), custom_call_target="Cholesky" | custom-call | tf_op jit(solution)/shard_map/jit(cholesky)/cholesky | solution.py:33
  530.6 9.8 %custom-call.33 = f32[1,128,128]{1,2,0:T(8,128)S(1)} custom-call(f32[1,128,128]{2,1,0:T(8,128)S(1)} %get-tuple-element.64), custom_call_target="InvertDiagBlocksLowerTriangular" | custom-call | tf_op jit(solution)/shard_map/jit(cholesky)/cholesky | solution.py:33
  542.7 11.7 %cholesky.343 = f32[128,128]{1,0:T(8,128)S(1)} custom-call(f32[128,128]{1,0:T(8,128)S(1)} %convolution_subtract_fusion.10), custom_call_target="Cholesky" | custom-call | tf_op jit(solution)/shard_map/jit(cholesky)/cholesky | solution.py:33
  560.7 11.6 %while.2 = (s32[]{:T(128)}, f32[512,512]{1,0:T(8,128)}, s32[4,2]{0,1:T(2,128)S(1)}, f32[4,128,128]{2,1,0:T(8,128)S(1)}, s32[]{:T(128)}) while((s32[]{:T(128)}, f32[512,512]{1,0:T(8,128)}, s32[4,2]{0,1:T(2,128)S(1)}, f32[4,128,128]{2,1,0:T(8,128)S(1)}, s32[]{:T(128)}) %tuple.70), condition=%wide.while_cond, body=%wide.while_body.sunk | while | flops 2 | bytes 131181 | solution.py:34
  572.2 40.2 %custom-call.26 = f32[4,128,128]{1,2,0:T(8,128)} custom-call(f32[4,128,128]{2,1,0:T(8,128)S(1)} %get-tuple-element.14), custom_call_target="InvertDiagBlocksLowerTriangular" | custom-call | tf_op jit(solution)/shard_map/triangular_solve | solution.py:34
  621.6 7.1 fusion.47
  628.7 231.0 %all-reduce.9.cloned.1.call-done = (f32[512,3072]{1,0:T(8,128)}, f32[512,384]{1,0:T(8,128)}) async-done(((f32[512,3072]{1,0:T(8,128)}, f32[512,384]{1,0:T(8,128)}), (f32[512,3072]{1,0:T(8,128)}, f32[512,384]{1,0:T(8,128)})) %all-reduce.9.cloned.1.call-update) | async-done | bytes 7077904 | tf_op jit(solution)/shard_map/psum | solution.py:37
  861.0 6.6 fusion.2
  868.1 6.6 all-reduce.3
  876.0 5.2 fusion.9
  885.8 5.4 fusion.1
  892.1 6.1 fusion
  (140 shorter events, 106.8 us)
Async XLA Ops:
  7.2 108.7 %all-gather.2.cloned.1.call-start = ((), (), s32[]{:S(2)}) async-start(), calls=%async_computation | async-start | bytes 7077888 | tf_op jit(solution)/shard_map/all_gather | solution.py:14
  7.9 170.6 %all-reduce.13.cloned.1.call-start = ((), (), s32[]{:S(2)}) async-start(), calls=%async_computation.3 | async-start | bytes 4456448 | tf_op jit(solution)/shard_map/psum | solution.py:18
  44.6 71.3 %copy-start.1 = (f32[192,3072]{1,0:T(8,128)S(1)}, f32[192,3072]{1,0:T(8,128)}, u32[]{:S(2)}) copy-start(f32[192,3072]{1,0:T(8,128)} %param.8) | copy-start | bytes 7077892
  126.6 162.3 %all-reduce.11.cloned.1.call-start = ((), (), s32[]{:S(2)}) async-start(), calls=%async_computation.2 | async-start | bytes 4194304 | tf_op jit(solution)/shard_map/psum | solution.py:28
  178.5 3.3 copy-start.4
  186.4 673.4 %all-reduce.9.cloned.1.call-start = ((), (), s32[]{:S(2)}) async-start(), calls=%async_computation.1 | async-start | bytes 14155776 | tf_op jit(solution)/shard_map/psum | solution.py:37
  288.9 5.2 copy-start.9
  297.4 1.0 copy-start.11
  322.5 0.7 copy-start.16
  445.6 4.4 copy-start.5
  453.1 8.4 copy-start.8
  453.1 4.2 copy-start.6
  453.1 4.2 copy-start.7
  457.3 4.2 copy-start.10
  612.4 9.2 %copy-start.2 = (f32[192,3072]{1,0:T(8,128)S(1)}, f32[192,3072]{1,0:T(8,128)}, u32[]{:S(2)}) copy-start(f32[192,3072]{1,0:T(8,128)} %param.7) | copy-start | bytes 7077892
  618.3 2.6 copy-start.12
  620.9 0.6 copy-start.14
  861.0 6.6 copy-start
  876.0 16.1 %slice-start = ((s8[6291456]{0:T(1024)(128)(4,1)}), s8[4194304]{0:T(1024)(128)(4,1)S(1)}, s32[]{:S(2)}) async-start(s8[6291456]{0:T(1024)(128)(4,1)} %bitcast.110), calls=%async_computation.4 | async-start | bytes 8388608
  881.9 3.8 copy-start.13
  881.9 3.8 copy-start.15
  881.9 10.2 %slice-start.1 = ((s8[6291456]{0:T(1024)(128)(4,1)}), s8[2097152]{0:T(1024)(128)(4,1)S(1)}, s32[]{:S(2)}) async-start(s8[6291456]{0:T(1024)(128)(4,1)} %bitcast.110), calls=%async_computation.5 | async-start | bytes 4194304
  885.7 6.4 copy-start.3
Sparse Core Ops, SparseCore 0:
  10.2 105.6 all-gather.1
  126.7 51.7 all-reduce.12
  186.5 102.3 all-reduce.10
  628.8 230.8 all-reduce.8
where the time goes:
time: 913 us; the launch traced here: 905 us
  waiting for transfers between devices  439 us (48%)
  other arithmetic  261 us (29%)
  matrix products  95.3 us (10%)
  blocking collectives  43.2 us (5%)
  local copies, waits for them, and re-layouts  34.8 us (4%)
  between operations  19.9 us (2%)
  starting transfers between devices  12 us (1%)
    psum x1, waiting for transfers between devices, finish(): lax.psum(jnp.dot(ortho.T, buffer, precision=highest, preferred_element_ty...  231 us
    another operation x30, other arithmetic, finish(): lower = jnp.linalg.cholesky(gram)  167 us
    psum x1, waiting for transfers between devices, single_gram(): return lax.psum(local_gram(proj), 'row')  102 us
    another operation x5, other arithmetic, finish(): lax.linalg.triangular_solve(lower, proj, left_side=False, lower=True, tra...  82.9 us
    all_gather x1, waiting for transfers between devices, project(): lax.all_gather(basis, 'row', axis=0, tiled=True)  65.1 us
    psum x1, waiting for transfers between devices, project(): return lax.psum(partial_proj, 'col')  40 us
    all_gather x1, blocking collectives, project(): lax.all_gather(basis, 'row', axis=0, tiled=True)  36.6 us
    another operation x24, local copies, waits for them, and re-layouts  23 us
  transfers between devices with their start and end apart: 4, of which 4 were waited for; matrix products, arithmetic and copies ran while one was open for 1% of the time, Pallas kernels for 0%

commit v1 on v0

--- a/solution.py
+++ b/solution.py
@@ -34,8 +34,11 @@
     ortho = lax.linalg.triangular_solve(lower, proj, left_side=False, lower=True, transpose_a=True)
     rank = ortho.shape[1]
     share_rows = rank // lax.axis_size("row")
-    trans = lax.psum(
-        jnp.dot(ortho.T, buffer, precision=highest, preferred_element_type=jnp.float32), "row"
+    trans = jnp.sum(
+        lax.all_gather(
+            jnp.dot(ortho.T, buffer, precision=highest, preferred_element_type=jnp.float32), "row"
+        ),
+        axis=0,
     )
     squares = lax.psum(jnp.sum(trans * trans, axis=1, keepdims=True), "col")
     full_basis = trans / jnp.sqrt(squares + EPS)

time: 913 us -> 1650 us (1.81)
  waiting for transfers between devices: 439 us -> 1150 us
  other arithmetic: 261 us -> 285 us
    all_gather x0 -> x2, waiting for transfers between devices: none -> 939 us  [finish(): lax.all_gather(jnp.dot(ortho.T, buffer, precision=highest, preferred_elem...]
    psum x1 -> x0, waiting for transfers between devices: 231 us -> none  [finish(): lax.psum(jnp.dot(ortho.T, buffer, precision=highest, preferred_element_ty...]
    reduce_sum x0 -> x2, other arithmetic: none -> 25.3 us  [finish(): jnp.sum(lax.all_gather(jnp.dot(ortho.T, buffer, precision=highest, prefer...]
  transfers between devices with their start and end apart: 4 -> 5, of which waited for: 4 -> 4; matrix products, arithmetic and copies ran while one was open for 1% -> 11% of each run, Pallas kernels for 0% -> 0%
where the time goes in v1:
time: 1650 us; the launch traced here: 1640 us
  waiting for transfers between devices  1150 us (70%)
  other arithmetic  285 us (17%)
  matrix products  94.9 us (6%)
  blocking collectives  43.2 us (3%)
  local copies, waits for them, and re-layouts  36.2 us (2%)
  between operations  19.6 us (1%)
    all_gather x2, waiting for transfers between devices, finish(): lax.all_gather(jnp.dot(ortho.T, buffer, precision=highest, preferred_elem...  939 us
    another operation x30, other arithmetic, finish(): lower = jnp.linalg.cholesky(gram)  167 us
    psum x1, waiting for transfers between devices, single_gram(): return lax.psum(local_gram(proj), 'row')  102 us
    another operation x5, other arithmetic, finish(): lax.linalg.triangular_solve(lower, proj, left_side=False, lower=True, tra...  82.7 us
    all_gather x1, waiting for transfers between devices, project(): lax.all_gather(basis, 'row', axis=0, tiled=True)  65.1 us
    psum x1, waiting for transfers between devices, project(): return lax.psum(partial_proj, 'col')  40 us
    all_gather x1, blocking collectives, project(): lax.all_gather(basis, 'row', axis=0, tiled=True)  36.6 us
  transfers between devices with their start and end apart: 5, of which 4 were waited for; matrix products, arithmetic and copies ran while one was open for 11% of the time, Pallas kernels for 0%

profile of v1, /device:TPU:0, one launch (start us, length us, event | category | flops | bytes accessed | tf_op | source)
XLA Modules:
  0.0 1639.5 jit_solution(7140545406466221056)
XLA Ops:
  7.9 36.6 %all_gather.21 = f32[512,384]{1,0:T(8,128)S(1)} all-gather(f32[64,384]{1,0:T(8,128)} %param.12), channel_id=1, replica_groups=mesh['row'=8,'col'=4] {'row'}, dimensions={0}, use_global_device_ids=true | all-gather | bytes 884736 | tf_op jit(solution)/shard_map/all_gather | solution.py:14
  44.6 6.2 fusion.76
  50.8 65.1 %all-gather.6.cloned.1.call-done = f32[512,3072]{1,0:T(8,128)} async-done(((f32[64,3072]{1,0:T(8,128)}), f32[512,3072]{1,0:T(8,128)}) %all-gather.6.cloned.1.call-update) | async-done | bytes 6291472 | tf_op jit(solution)/shard_map/all_gather | solution.py:14
  115.9 10.7 fusion.77
  126.6 11.9 all-reduce.7.cloned.1.call-start
  138.5 40.0 %all-reduce.9.cloned.1.call-done = (f32[192,512]{1,0:T(8,128)}, f32[896,512]{1,0:T(8,128)}) async-done(((f32[192,512]{1,0:T(8,128)}, f32[896,512]{1,0:T(8,128)}), (f32[192,512]{1,0:T(8,128)}, f32[896,512]{1,0:T(8,128)})) %all-reduce.9.cloned.1.call-update) | async-done | bytes 2228240 | tf_op jit(solution)/shard_map/psum | solution.py:18
  186.4 102.5 %all-reduce.7.cloned.1.call-done = (f32[512,512]{0,1:T(8,128)}, f32[512,512]{0,1:T(8,128)}) async-done(((f32[512,512]{0,1:T(8,128)}, f32[512,512]{0,1:T(8,128)}), (f32[512,512]{0,1:T(8,128)}, f32[512,512]{0,1:T(8,128)})) %all-reduce.7.cloned.1.call-update) | async-done | bytes 2097168 | tf_op jit(solution)/shard_map/psum | solution.py:28
  298.3 11.7 cholesky.358
  310.1 9.8 custom-call.34
  323.2 11.7 cholesky.377
  336.2 10.2 custom-call.35
  349.5 13.2 cholesky.398
  364.9 11.3 custom-call.36
  378.5 11.9 cholesky.415
  394.7 11.6 while.3
  406.3 39.3 %custom-call.27 = f32[4,128,128]{1,2,0:T(8,128)S(1)} custom-call(f32[4,128,128]{2,1,0:T(8,128)S(1)} %get-tuple-element.22), custom_call_target="InvertDiagBlocksLowerTriangular" | custom-call | tf_op jit(solution)/shard_map/triangular_solve | solution.py:34
  463.6 11.7 cholesky.286
  475.4 9.8 custom-call.31
  490.1 12.5 cholesky.305
  503.3 10.8 custom-call.32
  516.5 11.7 cholesky.326
  528.8 9.8 custom-call.33
  540.9 11.7 cholesky.343
  560.7 12.0 while.2
  572.7 39.9 %custom-call.26 = f32[4,128,128]{1,2,0:T(8,128)} custom-call(f32[4,128,128]{2,1,0:T(8,128)S(1)} %get-tuple-element.14), custom_call_target="InvertDiagBlocksLowerTriangular" | custom-call | tf_op jit(solution)/shard_map/triangular_solve | solution.py:34
  621.8 7.1 fusion.47
  634.3 6.9 fusion.2
  641.2 939.5 %all-gather.8.cloned.1.call-done = f32[4096,3072]{1,0:T(8,128)} async-done(((f32[512,3072]{1,0:T(8,128)}), f32[4096,3072]{1,0:T(8,128)}) %all-gather.8.cloned.1.call-update) | async-done | bytes 50331664 | tf_op jit(solution)/shard_map/all_gather | solution.py:38
  1580.7 21.2 %reduce_sum.36 = f32[512,3072]{1,0:T(8,128)} reduce(f32[8,512,3072]{2,1,0:T(8,128)} %bitcast.112, f32[]{:T(128)} %constant.124.clone.1), dimensions={0}, to_apply=%region_10.12 | reduce | flops 11010048 | bytes 56623108 | tf_op jit(solution)/shard_map/reduce_sum | solution.py:37
  1605.2 6.6 all-reduce.2
  1620.4 5.4 fusion.1
  1626.7 6.1 fusion
  (140 shorter events, 116.6 us)
Async XLA Ops:
  7.2 108.7 %all-gather.6.cloned.1.call-start = ((), (), s32[]{:S(2)}) async-start(), calls=%async_computation | async-start | bytes 7077888 | tf_op jit(solution)/shard_map/all_gather | solution.py:14
  7.9 170.6 %all-reduce.9.cloned.1.call-start = ((), (), s32[]{:S(2)}) async-start(), calls=%async_computation.4 | async-start | bytes 4456448 | tf_op jit(solution)/shard_map/psum | solution.py:18
  44.6 71.3 %copy-start.1 = (f32[192,3072]{1,0:T(8,128)S(1)}, f32[192,3072]{1,0:T(8,128)}, u32[]{:S(2)}) copy-start(f32[192,3072]{1,0:T(8,128)} %param.8) | copy-start | bytes 7077892
  126.6 162.3 %all-reduce.7.cloned.1.call-start = ((), (), s32[]{:S(2)}) async-start(), calls=%async_computation.3 | async-start | bytes 4194304 | tf_op jit(solution)/shard_map/psum | solution.py:28
  178.5 3.3 copy-start.4
  186.4 442.7 %all-gather.10.cloned.1.call-start = ((), (), s32[]{:S(2)}) async-start(), calls=%async_computation.2 | async-start | bytes 7077888 | tf_op jit(solution)/shard_map/all_gather | solution.py:38
  288.9 5.2 copy-start.9
  297.4 1.0 copy-start.11
  322.5 0.7 copy-start.16
  445.6 4.4 copy-start.5
  453.1 4.2 copy-start.8
  453.1 4.9 copy-start.6
  453.1 4.9 copy-start.7
  457.3 0.8 copy-start.10
  462.3 1118.4 %all-gather.8.cloned.1.call-start = ((), (), s32[]{:S(2)}) async-start(), calls=%async_computation.1 | async-start | bytes 56623104 | tf_op jit(solution)/shard_map/all_gather | solution.py:38
  612.7 9.2 copy-start.2
  618.6 2.6 copy-start.12
  621.2 0.6 copy-start.14
  1611.8 7.5 copy-start
  1619.3 1.0 copy-start.13
  1619.3 1.0 copy-start.15
  1620.3 6.4 copy-start.3
Sparse Core Ops, SparseCore 0:
  10.2 105.6 all-gather.5
  126.7 51.7 all-reduce.8
  186.5 102.3 all-reduce.6
  462.4 98.1 all-gather.9
  629.1 951.5 all-gather.7
